TPU v7x, 32 devices: a whole 2x2x4 slice. The times are simulated.
32 devices in a mesh: samp: 16 (over z, y, x), tm: 2 (over core).
Axes of the slice: x: 2, y: 2, z: 4, core: 2. Of those that a mesh axis runs over, the one named last changes fastest.
Arguments:
- sources: bfloat16 [256, 128, 1024], P('samp', 'tm'), may hold values from -6 to 6
- operator: bfloat16 [16, 1024, 128], P(None, 'samp'), may hold values from -0.046875 to 0.046875
- lag_order: int32 [16], replicated, may hold values from 0 to 15, each once
Outputs:
- records: bfloat16 [256, 128, 128], P('samp', 'tm')
Inputs may be any that keep to these rules, and one draw needn't show every extreme that they name: `lag_order`: each lag 0 to 15 stands in exactly one slot.
All inputs are finite; a program needn't handle non-finite values.
Results may differ from a plain program's by a relative error of at most 0.001.
Values may be sent and summed in bfloat16 or wider, within the bound.
A program may use at most 64 MiB of HBM per device.

v0:
```python
import jax
import jax.numpy as jnp
from jax import lax
from jax.sharding import PartitionSpec as P


def shifted_2(block, axis, distance):
    devices = range(lax.axis_size(axis))
    route = [(i - distance, i) for i in devices if i - distance in devices]
    return lax.ppermute(block, axis, route)


def accumulate(total, piece, extended, lag_order):
    border = piece.shape[0] - 1
    window = extended.shape[1] - border
    batch = extended.shape[0]
    width = piece.shape[1]

    def step(slot, state):
        lag = lag_order[slot]
        block = lax.dynamic_index_in_dim(piece, slot, 0, keepdims=False)
        shifted = lax.dynamic_slice(extended, (0, border - lag, 0), (batch, window, width))
        return state + jnp.einsum("btj,js->bts", shifted, block, preferred_element_type=jnp.float32)

    return lax.fori_loop(0, piece.shape[0], step, total)


def per_device(sources, operator, lag_order):
    batch, window, width = sources.shape
    border = operator.shape[0] - 1
    sensors = operator.shape[2]
    tail = sources[:, window - border :, :]
    before = shifted_2(tail, "tm", 1)
    extended = jnp.concatenate([before, sources], axis=1)
    init = jnp.zeros((batch, window, sensors), jnp.float32)
    gathered = lax.all_gather(operator, "samp", axis=1, tiled=True)
    total = accumulate(init, gathered, extended, lag_order)
    return total.astype(jnp.bfloat16)


def solution(mesh):
    placed = (P("samp", "tm", None), P(None, "samp", None), P())
    return jax.shard_map(
        per_device, mesh=mesh, in_specs=placed, out_specs=P("samp", "tm", None), check_vma=False
    )
```

profile of v0, /device:TPU:0, one launch (start us, length us, event | category | flops | bytes accessed | tf_op | source)
XLA Modules:
  0.0 154.3 jit_solution(4135805747650893638)
XLA Ops:
  6.5 0.0 all-gather.2.cloned.1.call-start
  6.5 0.7 all-gather.2.cloned.1.call-update
  7.3 1.2 slice.3
  8.5 3.2 %collective-permute-start = (bf16[16,15,1024]{2,1,0:T(8,128)(2,1)S(1)}, bf16[16,15,1024]{2,1,0:T(8,128)(2,1)}, u32[]{:S(2)}, u32[]{:S(2)}) collective-permute-start(bf16[16,15,1024]{2,1,0:T(8,128)(2,1)S(1)} %slice.3), channel_id=1, source_target_pairs={{0,1},{2,3},{4,5},{6,7},{8,9},{10,11},{12,13},{14,15},{16,17},{18,... | collective-permute-start | bytes 1474568 | tf_op jit(solution)/shard_map/ppermute | solution.py:10
  11.6 0.0 copy-start
  11.6 0.8 collective-permute-done
  12.5 2.6 %pad_maximum_fusion = bf16[16,79,1024]{2,1,0:T(8,128)(2,1)S(1)} fusion(bf16[16,64,1024]{2,1,0:T(8,128)(2,1)} %param.5, bf16[16,15,1024]{2,1,0:T(8,128)(2,1)} %collective-permute-done), kind=kLoop, calls=%fused_computation.6 | loop fusion | flops 5177344 | bytes 5177344 | tf_op jit(solution)/shard_map/concatenate | solution.py:34
  15.1 74.2 %all-gather.2.cloned.1.call-done = bf16[16,1024,128]{2,1,0:T(8,128)(2,1)} async-done(((bf16[16,64,128]{2,1,0:T(8,128)(2,1)}), bf16[16,1024,128]{2,1,0:T(8,128)(2,1)}) %all-gather.2.cloned.1.call-update) | async-done | bytes 4194320 | tf_op jit(solution)/shard_map/all_gather | solution.py:36
  89.2 0.0 copy-done
  89.2 57.5 %while.16 = (s32[]{:T(128)}, f32[16,64,128]{2,1,0:T(8,128)S(1)}, s32[16]{0:T(128)S(1)}, bf16[16,79,1024]{2,1,0:T(8,128)(2,1)S(1)}, bf16[16,1024,128]{2,1,0:T(8,1...) while((s32[]{:T(128)}, f32[16,64,128]{2,1,0:T(8,128)S(1)}, s32[16]{0:T(128)S(1)}, ...), condition=%wide.region_1.2_spmd.clone, body=%wide.region_0.1_spmd.clone.sunk | while | flops 268697600 | bytes 3408549 | solution.py:25
  89.2 0.6 dynamic_slice.47
  91.1 1.7 %fusion.13 = f32[16,64,128]{2,1,0:T(8,128)S(1)} fusion(bf16[16,79,1024]{2,1,0:T(8,128)(2,1)S(1)} %get-tuple-element.218, s32[]{:T(128)S(6)} %select_n.22, f32[16,64,128]{2,1,0:T(8,128)S(1)} %get-tuple-element.207, bf16[16,1024,128]{2,1,0:T(8,128)(2,1)} %get-tuple-element.219, s32[]{:T(128)} %get-tuple-element.206, pred[]{:T(512)S(6)} %compare.3), kind=kOutput, calls=%fused_computation.2.clone.1 | convolution fusion | flops 268697600 | bytes 3408389 | tf_op jit(solution)/shard_map/while/body/eval_jaxpr/btj,js->bts/dot_general | solution.py:23
  92.8 0.6 dynamic_slice.47
  94.7 1.7 %fusion.13 = f32[16,64,128]{2,1,0:T(8,128)S(1)} fusion(bf16[16,79,1024]{2,1,0:T(8,128)(2,1)S(1)} %get-tuple-element.218, s32[]{:T(128)S(6)} %select_n.22, f32[16,64,128]{2,1,0:T(8,128)S(1)} %get-tuple-element.207, bf16[16,1024,128]{2,1,0:T(8,128)(2,1)} %get-tuple-element.219, s32[]{:T(128)} %get-tuple-element.206, pred[]{:T(512)S(6)} %compare.3), kind=kOutput, calls=%fused_computation.2.clone.1 | convolution fusion | flops 268697600 | bytes 3408389 | tf_op jit(solution)/shard_map/while/body/eval_jaxpr/btj,js->bts/dot_general | solution.py:23
  96.4 0.6 dynamic_slice.47
  98.3 1.7 %fusion.13 = f32[16,64,128]{2,1,0:T(8,128)S(1)} fusion(bf16[16,79,1024]{2,1,0:T(8,128)(2,1)S(1)} %get-tuple-element.218, s32[]{:T(128)S(6)} %select_n.22, f32[16,64,128]{2,1,0:T(8,128)S(1)} %get-tuple-element.207, bf16[16,1024,128]{2,1,0:T(8,128)(2,1)} %get-tuple-element.219, s32[]{:T(128)} %get-tuple-element.206, pred[]{:T(512)S(6)} %compare.3), kind=kOutput, calls=%fused_computation.2.clone.1 | convolution fusion | flops 268697600 | bytes 3408389 | tf_op jit(solution)/shard_map/while/body/eval_jaxpr/btj,js->bts/dot_general | solution.py:23
  100.0 0.6 dynamic_slice.47
  101.8 1.7 %fusion.13 = f32[16,64,128]{2,1,0:T(8,128)S(1)} fusion(bf16[16,79,1024]{2,1,0:T(8,128)(2,1)S(1)} %get-tuple-element.218, s32[]{:T(128)S(6)} %select_n.22, f32[16,64,128]{2,1,0:T(8,128)S(1)} %get-tuple-element.207, bf16[16,1024,128]{2,1,0:T(8,128)(2,1)} %get-tuple-element.219, s32[]{:T(128)} %get-tuple-element.206, pred[]{:T(512)S(6)} %compare.3), kind=kOutput, calls=%fused_computation.2.clone.1 | convolution fusion | flops 268697600 | bytes 3408389 | tf_op jit(solution)/shard_map/while/body/eval_jaxpr/btj,js->bts/dot_general | solution.py:23
  103.6 0.6 dynamic_slice.47
  105.4 1.7 %fusion.13 = f32[16,64,128]{2,1,0:T(8,128)S(1)} fusion(bf16[16,79,1024]{2,1,0:T(8,128)(2,1)S(1)} %get-tuple-element.218, s32[]{:T(128)S(6)} %select_n.22, f32[16,64,128]{2,1,0:T(8,128)S(1)} %get-tuple-element.207, bf16[16,1024,128]{2,1,0:T(8,128)(2,1)} %get-tuple-element.219, s32[]{:T(128)} %get-tuple-element.206, pred[]{:T(512)S(6)} %compare.3), kind=kOutput, calls=%fused_computation.2.clone.1 | convolution fusion | flops 268697600 | bytes 3408389 | tf_op jit(solution)/shard_map/while/body/eval_jaxpr/btj,js->bts/dot_general | solution.py:23
  107.2 0.6 dynamic_slice.47
  109.0 1.7 %fusion.13 = f32[16,64,128]{2,1,0:T(8,128)S(1)} fusion(bf16[16,79,1024]{2,1,0:T(8,128)(2,1)S(1)} %get-tuple-element.218, s32[]{:T(128)S(6)} %select_n.22, f32[16,64,128]{2,1,0:T(8,128)S(1)} %get-tuple-element.207, bf16[16,1024,128]{2,1,0:T(8,128)(2,1)} %get-tuple-element.219, s32[]{:T(128)} %get-tuple-element.206, pred[]{:T(512)S(6)} %compare.3), kind=kOutput, calls=%fused_computation.2.clone.1 | convolution fusion | flops 268697600 | bytes 3408389 | tf_op jit(solution)/shard_map/while/body/eval_jaxpr/btj,js->bts/dot_general | solution.py:23
  110.8 0.6 dynamic_slice.47
  112.6 1.7 %fusion.13 = f32[16,64,128]{2,1,0:T(8,128)S(1)} fusion(bf16[16,79,1024]{2,1,0:T(8,128)(2,1)S(1)} %get-tuple-element.218, s32[]{:T(128)S(6)} %select_n.22, f32[16,64,128]{2,1,0:T(8,128)S(1)} %get-tuple-element.207, bf16[16,1024,128]{2,1,0:T(8,128)(2,1)} %get-tuple-element.219, s32[]{:T(128)} %get-tuple-element.206, pred[]{:T(512)S(6)} %compare.3), kind=kOutput, calls=%fused_computation.2.clone.1 | convolution fusion | flops 268697600 | bytes 3408389 | tf_op jit(solution)/shard_map/while/body/eval_jaxpr/btj,js->bts/dot_general | solution.py:23
  114.4 0.6 dynamic_slice.47
  116.2 1.7 %fusion.13 = f32[16,64,128]{2,1,0:T(8,128)S(1)} fusion(bf16[16,79,1024]{2,1,0:T(8,128)(2,1)S(1)} %get-tuple-element.218, s32[]{:T(128)S(6)} %select_n.22, f32[16,64,128]{2,1,0:T(8,128)S(1)} %get-tuple-element.207, bf16[16,1024,128]{2,1,0:T(8,128)(2,1)} %get-tuple-element.219, s32[]{:T(128)} %get-tuple-element.206, pred[]{:T(512)S(6)} %compare.3), kind=kOutput, calls=%fused_computation.2.clone.1 | convolution fusion | flops 268697600 | bytes 3408389 | tf_op jit(solution)/shard_map/while/body/eval_jaxpr/btj,js->bts/dot_general | solution.py:23
  118.0 0.6 dynamic_slice.47
  119.8 1.7 %fusion.13 = f32[16,64,128]{2,1,0:T(8,128)S(1)} fusion(bf16[16,79,1024]{2,1,0:T(8,128)(2,1)S(1)} %get-tuple-element.218, s32[]{:T(128)S(6)} %select_n.22, f32[16,64,128]{2,1,0:T(8,128)S(1)} %get-tuple-element.207, bf16[16,1024,128]{2,1,0:T(8,128)(2,1)} %get-tuple-element.219, s32[]{:T(128)} %get-tuple-element.206, pred[]{:T(512)S(6)} %compare.3), kind=kOutput, calls=%fused_computation.2.clone.1 | convolution fusion | flops 268697600 | bytes 3408389 | tf_op jit(solution)/shard_map/while/body/eval_jaxpr/btj,js->bts/dot_general | solution.py:23
  121.6 0.6 dynamic_slice.47
  123.4 1.7 %fusion.13 = f32[16,64,128]{2,1,0:T(8,128)S(1)} fusion(bf16[16,79,1024]{2,1,0:T(8,128)(2,1)S(1)} %get-tuple-element.218, s32[]{:T(128)S(6)} %select_n.22, f32[16,64,128]{2,1,0:T(8,128)S(1)} %get-tuple-element.207, bf16[16,1024,128]{2,1,0:T(8,128)(2,1)} %get-tuple-element.219, s32[]{:T(128)} %get-tuple-element.206, pred[]{:T(512)S(6)} %compare.3), kind=kOutput, calls=%fused_computation.2.clone.1 | convolution fusion | flops 268697600 | bytes 3408389 | tf_op jit(solution)/shard_map/while/body/eval_jaxpr/btj,js->bts/dot_general | solution.py:23
  125.2 0.6 dynamic_slice.47
  127.0 1.7 %fusion.13 = f32[16,64,128]{2,1,0:T(8,128)S(1)} fusion(bf16[16,79,1024]{2,1,0:T(8,128)(2,1)S(1)} %get-tuple-element.218, s32[]{:T(128)S(6)} %select_n.22, f32[16,64,128]{2,1,0:T(8,128)S(1)} %get-tuple-element.207, bf16[16,1024,128]{2,1,0:T(8,128)(2,1)} %get-tuple-element.219, s32[]{:T(128)} %get-tuple-element.206, pred[]{:T(512)S(6)} %compare.3), kind=kOutput, calls=%fused_computation.2.clone.1 | convolution fusion | flops 268697600 | bytes 3408389 | tf_op jit(solution)/shard_map/while/body/eval_jaxpr/btj,js->bts/dot_general | solution.py:23
  128.8 0.6 dynamic_slice.47
  130.6 1.7 %fusion.13 = f32[16,64,128]{2,1,0:T(8,128)S(1)} fusion(bf16[16,79,1024]{2,1,0:T(8,128)(2,1)S(1)} %get-tuple-element.218, s32[]{:T(128)S(6)} %select_n.22, f32[16,64,128]{2,1,0:T(8,128)S(1)} %get-tuple-element.207, bf16[16,1024,128]{2,1,0:T(8,128)(2,1)} %get-tuple-element.219, s32[]{:T(128)} %get-tuple-element.206, pred[]{:T(512)S(6)} %compare.3), kind=kOutput, calls=%fused_computation.2.clone.1 | convolution fusion | flops 268697600 | bytes 3408389 | tf_op jit(solution)/shard_map/while/body/eval_jaxpr/btj,js->bts/dot_general | solution.py:23
  132.4 0.6 dynamic_slice.47
  134.2 1.7 %fusion.13 = f32[16,64,128]{2,1,0:T(8,128)S(1)} fusion(bf16[16,79,1024]{2,1,0:T(8,128)(2,1)S(1)} %get-tuple-element.218, s32[]{:T(128)S(6)} %select_n.22, f32[16,64,128]{2,1,0:T(8,128)S(1)} %get-tuple-element.207, bf16[16,1024,128]{2,1,0:T(8,128)(2,1)} %get-tuple-element.219, s32[]{:T(128)} %get-tuple-element.206, pred[]{:T(512)S(6)} %compare.3), kind=kOutput, calls=%fused_computation.2.clone.1 | convolution fusion | flops 268697600 | bytes 3408389 | tf_op jit(solution)/shard_map/while/body/eval_jaxpr/btj,js->bts/dot_general | solution.py:23
  136.0 0.6 dynamic_slice.47
  137.8 1.7 %fusion.13 = f32[16,64,128]{2,1,0:T(8,128)S(1)} fusion(bf16[16,79,1024]{2,1,0:T(8,128)(2,1)S(1)} %get-tuple-element.218, s32[]{:T(128)S(6)} %select_n.22, f32[16,64,128]{2,1,0:T(8,128)S(1)} %get-tuple-element.207, bf16[16,1024,128]{2,1,0:T(8,128)(2,1)} %get-tuple-element.219, s32[]{:T(128)} %get-tuple-element.206, pred[]{:T(512)S(6)} %compare.3), kind=kOutput, calls=%fused_computation.2.clone.1 | convolution fusion | flops 268697600 | bytes 3408389 | tf_op jit(solution)/shard_map/while/body/eval_jaxpr/btj,js->bts/dot_general | solution.py:23
  139.6 0.6 dynamic_slice.47
  141.4 1.7 %fusion.13 = f32[16,64,128]{2,1,0:T(8,128)S(1)} fusion(bf16[16,79,1024]{2,1,0:T(8,128)(2,1)S(1)} %get-tuple-element.218, s32[]{:T(128)S(6)} %select_n.22, f32[16,64,128]{2,1,0:T(8,128)S(1)} %get-tuple-element.207, bf16[16,1024,128]{2,1,0:T(8,128)(2,1)} %get-tuple-element.219, s32[]{:T(128)} %get-tuple-element.206, pred[]{:T(512)S(6)} %compare.3), kind=kOutput, calls=%fused_computation.2.clone.1 | convolution fusion | flops 268697600 | bytes 3408389 | tf_op jit(solution)/shard_map/while/body/eval_jaxpr/btj,js->bts/dot_general | solution.py:23
  143.2 0.6 dynamic_slice.47
  145.0 1.7 %fusion.13 = f32[16,64,128]{2,1,0:T(8,128)S(1)} fusion(bf16[16,79,1024]{2,1,0:T(8,128)(2,1)S(1)} %get-tuple-element.218, s32[]{:T(128)S(6)} %select_n.22, f32[16,64,128]{2,1,0:T(8,128)S(1)} %get-tuple-element.207, bf16[16,1024,128]{2,1,0:T(8,128)(2,1)} %get-tuple-element.219, s32[]{:T(128)} %get-tuple-element.206, pred[]{:T(512)S(6)} %compare.3), kind=kOutput, calls=%fused_computation.2.clone.1 | convolution fusion | flops 268697600 | bytes 3408389 | tf_op jit(solution)/shard_map/while/body/eval_jaxpr/btj,js->bts/dot_general | solution.py:23
  146.8 0.7 convert_element_type.3
  (1 shorter events, 0.0 us)
Async XLA Ops:
  6.5 82.7 %all-gather.2.cloned.1.call-start = ((), (), s32[]{:S(2)}) async-start(), calls=%async_computation | async-start | bytes 4456448 | tf_op jit(solution)/shard_map/all_gather | solution.py:36
  8.5 4.0 %collective-permute-start = (bf16[16,15,1024]{2,1,0:T(8,128)(2,1)S(1)}, bf16[16,15,1024]{2,1,0:T(8,128)(2,1)}, u32[]{:S(2)}, u32[]{:S(2)}) collective-permute-start(bf16[16,15,1024]{2,1,0:T(8,128)(2,1)S(1)} %slice.3), channel_id=1, source_target_pairs={{0,1},{2,3},{4,5},{6,7},{8,9},{10,11},{12,13},{14,15},{16,17},{18,... | collective-permute-start | bytes 1474568 | tf_op jit(solution)/shard_map/ppermute | solution.py:10
  11.6 77.6 %copy-start = (s32[16]{0:T(128)S(1)}, s32[16]{0:T(128)}, u32[]{:S(2)}) copy-start(s32[16]{0:T(128)} %param.7) | copy-start | bytes 196
Sparse Core Ops, SparseCore 0:
  10.1 79.0 all-gather.1
where the time goes:
time: 155 us; the launch traced here: 154 us
  waiting for transfers between devices  75.7 us (49%)
  matrix products  27.8 us (18%)
  loops' own time  20.2 us (13%)
  between operations  13.4 us (9%)
  local copies, waits for them, and re-layouts  10.7 us (7%)
  other arithmetic  3.33 us (2%)
  starting transfers between devices  3.18 us (2%)
    all_gather x1, waiting for transfers between devices, per_device(): gathered = lax.all_gather(operator, 'samp', axis=1, tiled=True)  74.2 us
    dot_general x16, matrix products, step(): jnp.einsum('btj,js->bts', shifted, block, preferred_element_type=jnp.floa...  27.8 us
    another operation x1, loops' own time, accumulate(): return lax.fori_loop(0, piece.shape[0], step, total)  20.2 us
    dynamic_slice x16, local copies, waits for them, and re-layouts, step(): lag = lag_order[slot]  9.47 us
    ppermute x1, starting transfers between devices, shifted_2(): return lax.ppermute(block, axis, route)  3.17 us
  transfers between devices with their start and end apart: 2, of which 2 were waited for; matrix products, arithmetic and copies ran while one was open for 2% of the time, Pallas kernels for 0%

commit v1 on v0

v1 whole, which is shorter than its diff:
```python
import functools
import math

import jax
import jax.numpy as jnp
from jax import lax
from jax.experimental import pallas as pl
from jax.experimental.pallas import tpu as pltpu
from jax.sharding import PartitionSpec as P

MESH = pl.DeviceIdType.MESH
HALO = 16
Z, A, B = 0, 1, 2
ORDERS = ((Z, A, B), (B, Z, A))


def when(cond, fn):
    if cond is True:
        fn()
    elif cond is not False:
        pl.when(cond)(fn)


def ranked(me, size, rank):
    if rank == 0:
        return me, None
    if size == 2:
        return 1 - me, None
    low = jnp.minimum(me, size - 1 - me)
    side = 1 - 2 * (me // ((size + 1) // 2))
    alternate = (rank + 1) // 2 if rank % 2 else -((rank + 1) // 2)
    near = rank <= 2 * low
    offset = side * jnp.where(near, alternate, rank - low)
    away = side * jnp.where(near, -1 if rank % 2 else 1, -1)
    return me + offset, away


def fused(sizes, n_tm, lags, src_hbm, op_ref, lag_ref, out_ref,
          xin, halo, xt, w, acc, in_sem, halo_send, halo_recv, send_sem, recv_sem):
    planes, side_size, _ = sizes
    batch, window, _ = xin.shape
    depth = op_ref.shape[1]
    sensors = op_ref.shape[2]
    pairs = lags // 2
    piece = pairs // 4
    width = side_size * side_size * depth
    samp = lax.axis_index("samp")
    tm = lax.axis_index("tm")
    core = tm % 2
    sibling = tm + 1 - 2 * core
    z = samp // (side_size * side_size)
    y = (samp // side_size) % side_size
    x = samp % side_size
    a = x + core * (y - x)
    b = y + core * (x - y)
    stride_a = 1 + core * (side_size - 1)
    stride_b = side_size - core * (side_size - 1)
    me = (z, a, b)

    def flat(at):
        return at[Z] * (side_size * side_size) + at[A] * stride_a + at[B] * stride_b

    def both(d):
        if sizes[d] == 1:
            return []
        if sizes[d] == 2:
            return [(True, 1 - me[d])]
        return [(me[d] > 0, me[d] - 1), (me[d] < sizes[d] - 1, me[d] + 1)]

    def moved(d, to):
        at = list(me)
        at[d] = to
        return flat(at)

    load = pltpu.make_async_copy(src_hbm, xin, in_sem)
    load.start()

    barrier = pltpu.get_barrier_semaphore()
    expected = 1
    pl.semaphore_signal(barrier, inc=1, device_id=(samp, sibling), device_id_type=MESH)
    for d in (Z, A, B):
        for cond, to in both(d):
            when(cond, lambda d=d, to=to: pl.semaphore_signal(
                barrier, inc=1, device_id=(moved(d, to), tm), device_id_type=MESH))
            expected = expected + (1 if cond is True else cond.astype(jnp.int32))
    for cond, to in ((tm > 0, tm - 1), (tm < n_tm - 1, tm + 1)):
        when(cond, lambda to=to: pl.semaphore_signal(
            barrier, inc=1, device_id=(samp, to), device_id_type=MESH))
        expected = expected + cond.astype(jnp.int32)

    own_rows = pl.multiple_of((samp % (side_size * side_size)) * depth, depth)
    for lag in range(lags):
        slot = jnp.int32(0)
        for k in range(lags):
            slot = jnp.where(lag_ref[k] == lag, k, slot)
        w[z, lag // 2, pl.ds(own_rows, depth), (lag % 2) * sensors:(lag % 2 + 1) * sensors] = op_ref[slot]

    pl.semaphore_wait(barrier, expected)

    def block(at, q, of_core):
        rows = pl.multiple_of((flat(at) - at[Z] * (side_size * side_size)) * depth, depth)
        return w.at[at[Z], pl.ds((2 * of_core + q) * piece, piece), pl.ds(rows, depth), :]

    def copy(at, q, slot, device):
        ref = block(at, q, core)
        source = flat(at)
        return pltpu.make_async_remote_copy(
            src_ref=ref, dst_ref=ref,
            send_sem=send_sem.at[q, slot, source],
            recv_sem=recv_sem.at[1 if slot == 6 else 0, q, source],
            device_id=device, device_id_type=MESH)

    sends = []

    def send(cond, at, q, slot, device):
        when(cond, lambda: copy(at, q, slot, device).start())
        sends.append((cond, at, q, slot, device))

    def await_block(at, q, slot):
        copy(at, q, slot, (samp, sibling)).wait_recv()

    def sibling_wait(at, q):
        ref = block(at, q, 1 - core)
        pltpu.make_async_remote_copy(
            src_ref=ref, dst_ref=ref,
            send_sem=send_sem.at[q, 6, flat(at)],
            recv_sem=recv_sem.at[1, q, flat(at)],
            device_id=(samp, sibling), device_id_type=MESH).wait_recv()

    def process(ranks, q):
        order = ORDERS[q]
        spots = [ranked(me[d], sizes[d], ranks[d]) for d in (Z, A, B)]
        at = tuple(s[0] for s in spots)
        last = -1
        for i, d in enumerate(order):
            if ranks[d]:
                last = i
        if last >= 0:
            await_block(at, q, 0)
            d = order[last]
            away = spots[d][1]
            if away is not None:
                to = me[d] + away
                send((to >= 0) & (to < sizes[d]), at, q, 2 * d, (moved(d, to), tm))
        for d in order[last + 1:]:
            for i, (cond, to) in enumerate(both(d)):
                send(cond, at, q, 2 * d + i, (moved(d, to), tm))
        if last >= 0:
            send(True, at, q, 6, (samp, sibling))

    flips = [(i, j) for i in range(side_size) for j in range(side_size)]
    flips.sort(key=sum)

    for q in range(2):
        process((0, 0, 0), q)

    tail = pltpu.make_async_remote_copy(
        src_ref=src_hbm.at[:, pl.ds(window - HALO, HALO), :], dst_ref=halo,
        send_sem=halo_send, recv_sem=halo_recv,
        device_id=(samp, lax.rem(tm + 1, n_tm)), device_id_type=MESH)
    pl.when(tm < n_tm - 1)(tail.start)

    square = batch * HALO
    row = lax.broadcasted_iota(jnp.int32, (square, square), 0)
    col = lax.broadcasted_iota(jnp.int32, (square, square), 1)
    to_time = (col == (row % batch) * HALO + row // batch).astype(jnp.bfloat16)
    to_batch = (col == (row % HALO) * batch + row // HALO).astype(jnp.bfloat16)

    def turn(values, first):
        values = values.reshape(square, values.shape[-1])
        for p in range(planes):
            part = jnp.dot(to_time, values[:, p * width:(p + 1) * width],
                           preferred_element_type=jnp.float32).astype(jnp.bfloat16)
            xt[p, first:first + HALO] = part.reshape(HALO, batch, width)

    def turn_halo():
        @pl.when(tm > 0)
        def _():
            tail.wait_recv()
            turn(halo[...], 0)

        @pl.when(tm == 0)
        def _():
            xt[:, 0:HALO] = jnp.zeros((planes, HALO, batch, width), jnp.bfloat16)

    def unit(rank, pair, first):
        p = ranked(z, planes, rank)[0]
        lhs = xt[p, HALO - 1 - 2 * pair:HALO + window - 2 * pair].reshape((window + 1) * batch, width)
        part = jnp.dot(lhs, w[p, pair], preferred_element_type=jnp.float32)
        if first:
            acc[...] = part
        else:
            acc[...] += part

    def turn_own(i):
        if i == 0:
            load.wait()
        turn(xin[:, i * HALO:(i + 1) * HALO, :], HALO + i * HALO)

    work = [functools.partial(turn_own, i) for i in range(window // HALO)] + [turn_halo]
    for rank in range(planes):
        steps = [((rank, i, j), q) for i, j in flips for q in range(2) if (rank, i, j) != (0, 0, 0)]
        for n, (ranks, q) in enumerate(steps):
            process(ranks, q)
            for _ in range(-(-len(work) // (len(steps) - n))):
                if work:
                    work.pop(0)()
        while work:
            work.pop(0)()
        for ranks, q in steps:
            sibling_wait(tuple(ranked(me[d], sizes[d], ranks[d])[0] for d in (Z, A, B)), q)
        work = [functools.partial(unit, rank, pair, rank == 0 and pair == 0) for pair in range(pairs)]
    for item in work:
        item()

    total = (acc[batch:, :sensors] + acc[:window * batch, sensors:]).astype(jnp.bfloat16)
    for i in range(window // HALO):
        part = jnp.dot(to_batch, total[i * square:(i + 1) * square],
                       preferred_element_type=jnp.float32).astype(jnp.bfloat16)
        out_ref[:, i * HALO:(i + 1) * HALO, :] = part.reshape(batch, HALO, sensors)

    for cond, at, q, slot, device in sends:
        when(cond, lambda at=at, q=q, slot=slot, device=device: copy(at, q, slot, device).wait_send())
    pl.when(tm < n_tm - 1)(tail.wait_send)


def per_device(n_samp, n_tm, sources, operator, lag_order):
    batch, window, total_depth = sources.shape
    lags, depth, sensors = operator.shape
    side = math.isqrt(n_samp // 4)
    sizes = (n_samp // (side * side), side, side)
    width = side * side * depth
    return pl.pallas_call(
        functools.partial(fused, sizes, n_tm, lags),
        out_shape=jax.ShapeDtypeStruct((batch, window, sensors), jnp.bfloat16),
        in_specs=[
            pl.BlockSpec(memory_space=pl.ANY),
            pl.BlockSpec(memory_space=pltpu.VMEM),
            pl.BlockSpec(memory_space=pltpu.SMEM),
        ],
        out_specs=pl.BlockSpec(memory_space=pltpu.VMEM),
        scratch_shapes=[
            pltpu.VMEM((batch, window, total_depth), jnp.bfloat16),
            pltpu.VMEM((batch, HALO, total_depth), jnp.bfloat16),
            pltpu.VMEM((sizes[0], HALO + window, batch, width), jnp.bfloat16),
            pltpu.VMEM((sizes[0], lags // 2, width, 2 * sensors), jnp.bfloat16),
            pltpu.VMEM(((window + 1) * batch, 2 * sensors), jnp.float32),
            pltpu.SemaphoreType.DMA(()),
            pltpu.SemaphoreType.DMA(()),
            pltpu.SemaphoreType.DMA(()),
            pltpu.SemaphoreType.DMA((2, 7, n_samp)),
            pltpu.SemaphoreType.DMA((2, 2, n_samp)),
        ],
        compiler_params=pltpu.CompilerParams(
            collective_id=0, has_side_effects=True, vmem_limit_bytes=48 << 20),
    )(sources, operator, lag_order)


def solution(mesh):
    placed = (P("samp", "tm", None), P(None, "samp", None), P())
    return jax.shard_map(
        functools.partial(per_device, mesh.shape["samp"], mesh.shape["tm"]),
        mesh=mesh, in_specs=placed, out_specs=P("samp", "tm", None), check_vma=False,
    )
```

time: 155 us -> 52.4 us (0.34)
  waiting for transfers between devices: 75.7 us -> 0 us
  Pallas kernels: 0 us -> 47.8 us
  matrix products: 27.8 us -> 0 us
  loops' own time: 20.2 us -> 0 us
  between operations: 13.4 us -> 0.01 us
  local copies, waits for them, and re-layouts: 10.7 us -> 3.9 us
  other arithmetic: 3.33 us -> 0 us
  starting transfers between devices: 3.18 us -> 0 us
    all_gather x1 -> x0, waiting for transfers between devices: 74.2 us -> none  [per_device(): gathered = lax.all_gather(operator, 'samp', axis=1, tiled=True)]
    pallas_call x0 -> x1, Pallas kernels: none -> 47.8 us  [per_device(): pl.pallas_call(functools.partial(fused, sizes, n_tm, lags), out_shape=jax...]
    dot_general x16 -> x0, matrix products: 27.8 us -> none  [step(): jnp.einsum('btj,js->bts', shifted, block, preferred_element_type=jnp.floa...]
    another operation x1 -> x0, loops' own time: 20.2 us -> none  [accumulate(): return lax.fori_loop(0, piece.shape[0], step, total)]
    dynamic_slice x16 -> x0, local copies, waits for them, and re-layouts: 9.47 us -> none  [step(): lag = lag_order[slot]]
    unnamed x2 -> x7, local copies, waits for them, and re-layouts: 0.01 us -> 3.9 us
    ppermute x1 -> x0, starting transfers between devices: 3.17 us -> none  [shifted_2(): return lax.ppermute(block, axis, route)]
    concatenate x1 -> x0, other arithmetic: 2.58 us -> none  [per_device(): extended = jnp.concatenate([before, sources], axis=1)]
  transfers between devices with their start and end apart: 2 -> 0, of which waited for: 2 -> 0; matrix products, arithmetic and copies ran while one was open for 2% -> 0% of each run, Pallas kernels for 0% -> 0%
where the time goes in v1:
time: 52.4 us; the launch traced here: 51.7 us
  Pallas kernels  47.8 us (91%)
  local copies, waits for them, and re-layouts  3.9 us (7%)
    pallas_call x1, Pallas kernels, per_device(): pl.pallas_call(functools.partial(fused, sizes, n_tm, lags), out_shape=jax...  47.8 us
    unnamed x7, local copies, waits for them, and re-layouts  3.9 us

profile of v1, /device:TPU:0, one launch (start us, length us, event | category | flops | bytes accessed | tf_op | source)
XLA Modules:
  0.0 51.7 jit_solution(14205728672840157973)
XLA Ops:
  0.0 0.0 copy-start
  0.0 1.6 %copy-done = bf16[16,64,1024]{2,1,0:T(8,128)(2,1)S(1)} copy-done((bf16[16,64,1024]{2,1,0:T(8,128)(2,1)S(1)}, bf16[16,64,1024]{2,1,0:T(8,128)(2,1)}, u32[]{:S(2)}) %copy-start) | copy-done | bytes 2097176
  1.6 0.0 copy-start.1
  1.6 0.9 %copy-done.1 = bf16[16,64,128]{2,1,0:T(8,128)(2,1)S(1)} copy-done((bf16[16,64,128]{2,1,0:T(8,128)(2,1)S(1)}, bf16[16,64,128]{2,1,0:T(8,128)(2,1)}, u32[]{:S(2)}) %copy-start.1) | copy-done | bytes 262168
  2.5 0.0 copy-start.2
  2.5 0.7 %copy-done.2 = s32[16]{0:T(128)S(1)} copy-done((s32[16]{0:T(128)S(1)}, s32[16]{0:T(128)}, u32[]{:S(2)}) %copy-start.2) | copy-done | bytes 88
  3.2 47.8 %shard_map.37 = bf16[16,64,128]{2,1,0:T(8,128)(2,1)S(1)} custom-call(bf16[16,64,1024]{2,1,0:T(8,128)(2,1)S(1)} %copy-done, bf16[16,64,128]{2,1,0:T(8,128)(2,1)S(1)} %copy-done.1, s32[16]{0:T(128)S(1)} %copy-done.2), custom_call_target="tpu_custom_call" | custom-call | tf_op jit(solution)/shard_map/pallas_call | solution.py:233
  51.0 0.7 %copy.5 = bf16[16,64,128]{2,1,0:T(8,128)(2,1)} copy(bf16[16,64,128]{2,1,0:T(8,128)(2,1)S(1)} %shard_map.37) | data formatting | bytes 524288
Async XLA Ops:
  0.0 1.6 %copy-start = (bf16[16,64,1024]{2,1,0:T(8,128)(2,1)S(1)}, bf16[16,64,1024]{2,1,0:T(8,128)(2,1)}, u32[]{:S(2)}) copy-start(bf16[16,64,1024]{2,1,0:T(8,128)(2,1)} %src_hbm.1) | copy-start | bytes 6291460
  1.6 0.9 %copy-start.1 = (bf16[16,64,128]{2,1,0:T(8,128)(2,1)S(1)}, bf16[16,64,128]{2,1,0:T(8,128)(2,1)}, u32[]{:S(2)}) copy-start(bf16[16,64,128]{2,1,0:T(8,128)(2,1)} %op_ref.1) | copy-start | bytes 786436
  2.5 0.7 %copy-start.2 = (s32[16]{0:T(128)S(1)}, s32[16]{0:T(128)}, u32[]{:S(2)}) copy-start(s32[16]{0:T(128)} %lag_ref.1) | copy-start | bytes 196

commit v2 on v1

v2 whole, which is shorter than its diff:
```python
import functools
import math

import jax
import jax.numpy as jnp
from jax import lax
from jax.experimental import pallas as pl
from jax.experimental.pallas import tpu as pltpu
from jax.sharding import PartitionSpec as P

MESH = pl.DeviceIdType.MESH
HALO = 16
Z, A, B = 0, 1, 2
ORDERS = ((Z, A, B),)
SHARES = ((0, 4),)
HOP = 3
POPS = 2
LAST = 11


def ranked(me, size, rank):
    if rank == 0:
        return me
    if size == 2:
        return 1 - me
    low = jnp.minimum(me, size - 1 - me)
    side = 1 - 2 * (me // ((size + 1) // 2))
    alternate = (rank + 1) // 2 if rank % 2 else -((rank + 1) // 2)
    near = rank <= 2 * low
    return me + side * jnp.where(near, alternate, rank - low)


def fused(sizes, n_tm, lags, src_hbm, op_ref, lag_ref, out_ref,
          xin, halo, xt, w, acc, in_sem, halo_send, halo_recv, send_sem, recv_sem):
    planes, side_size, _ = sizes
    batch, window, _ = xin.shape
    depth = op_ref.shape[1]
    sensors = op_ref.shape[2]
    pairs = lags // 2
    width = side_size * side_size * depth
    samp = lax.axis_index("samp")
    tm = lax.axis_index("tm")
    core = tm % 2
    sibling = tm + 1 - 2 * core
    z = samp // (side_size * side_size)
    y = (samp // side_size) % side_size
    x = samp % side_size
    stride_a = 1 + core * (side_size - 1)
    stride_b = side_size - core * (side_size - 1)
    me = (z, x + core * (y - x), y + core * (x - y))

    def flat(at):
        return at[Z] * (side_size * side_size) + at[A] * stride_a + at[B] * stride_b

    places = [[ranked(me[d], sizes[d], rank) for rank in range(sizes[d])] for d in (Z, A, B)]

    def peer(d, rank):
        at = list(me)
        at[d] = places[d][rank]
        return (flat(at), tm)

    load = pltpu.make_async_copy(src_hbm, xin, in_sem)
    load.start()

    barrier = pltpu.get_barrier_semaphore()
    expected = 1 + sum(sizes) - 3
    pl.semaphore_signal(barrier, inc=1, device_id=(samp, sibling), device_id_type=MESH)
    for d in (Z, A, B):
        for rank in range(1, sizes[d]):
            pl.semaphore_signal(barrier, inc=1, device_id=peer(d, rank), device_id_type=MESH)
    for cond, to in ((tm > 0, tm - 1), (tm < n_tm - 1, tm + 1)):
        pl.when(cond)(functools.partial(
            pl.semaphore_signal, barrier, inc=1, device_id=(samp, to), device_id_type=MESH))
        expected = expected + cond.astype(jnp.int32)

    own_rows = pl.multiple_of((samp % (side_size * side_size)) * depth, depth)
    for lag in range(lags):
        slot = jnp.int32(0)
        for k in range(lags):
            slot = jnp.where(lag_ref[k] == lag, k, slot)
        w[z, lag // 2, pl.ds(own_rows, depth), (lag % 2) * sensors:(lag % 2 + 1) * sensors] = op_ref[slot]

    pl.semaphore_wait(barrier, expected)

    def copy(ranks, q, of_core, slot, device):
        at = [places[d][ranks[d]] for d in (Z, A, B)]
        source = flat(at)
        rows = pl.multiple_of((source - at[Z] * (side_size * side_size)) * depth, depth)
        first, count = SHARES[q]
        half = pairs // 2
        ref = w.at[at[Z], pl.ds(of_core * half + half * first // 4, half * count // 4), pl.ds(rows, depth), :]
        return pltpu.make_async_remote_copy(
            src_ref=ref, dst_ref=ref,
            send_sem=send_sem.at[q, slot, source],
            recv_sem=recv_sem.at[1 if slot == 0 else 0, q, source],
            device_id=device, device_id_type=MESH)

    sends = []

    def send(cond, *args):
        if cond is None:
            copy(*args).start()
        else:
            pl.when(cond)(lambda: copy(*args).start())
        sends.append((cond, args))

    relayed = planes == 4
    inner = (z > 0) & (z < planes - 1)

    def process(ranks, q):
        order = ORDERS[q]
        last = -1
        for i, d in enumerate(order):
            if ranks[d]:
                last = i
        if last >= 0:
            copy(ranks, q, core, 1, (samp, sibling)).wait_recv()
        slot = 1
        for d in (A, B, Z):
            for rank in range(1, sizes[d]):
                far = relayed and d == Z and rank == planes - 1
                if d in order[last + 1:]:
                    send(inner if far else None, ranks, q, core, slot, peer(d, rank))
                elif far and last >= 0 and order[last] == Z and ranks[Z] == rank:
                    at = (planes - 1 - places[Z][rank], me[A], me[B])
                    send(inner, ranks, q, core, slot, (flat(at), tm))
                slot += 1
        if last >= 0:
            send(None, ranks, q, core, 0, (samp, sibling))

    def sibling_wait(ranks, q):
        copy(ranks, q, 1 - core, 0, (samp, sibling)).wait_recv()

    for q in range(len(ORDERS)):
        process((0, 0, 0), q)

    tail = pltpu.make_async_remote_copy(
        src_ref=src_hbm.at[:, pl.ds(window - HALO, HALO), :], dst_ref=halo,
        send_sem=halo_send, recv_sem=halo_recv,
        device_id=(samp, lax.rem(tm + 1, n_tm)), device_id_type=MESH)
    pl.when(tm < n_tm - 1)(tail.start)

    square = batch * HALO
    row = lax.broadcasted_iota(jnp.int32, (square, square), 0)
    col = lax.broadcasted_iota(jnp.int32, (square, square), 1)
    to_time = (col == (row % batch) * HALO + row // batch).astype(jnp.bfloat16)
    to_batch = (col == (row % HALO) * batch + row // HALO).astype(jnp.bfloat16)

    def turn(values, first):
        values = values.reshape(square, values.shape[-1])
        for p in range(planes):
            part = jnp.dot(to_time, values[:, p * width:(p + 1) * width],
                           preferred_element_type=jnp.float32).astype(jnp.bfloat16)
            xt[p, first:first + HALO] = part.reshape(HALO, batch, width)

    def turn_halo():
        @pl.when(tm > 0)
        def _():
            tail.wait_recv()
            turn(halo[...], 0)

        @pl.when(tm == 0)
        def _():
            xt[:, 0:HALO] = jnp.zeros((planes, HALO, batch, width), jnp.bfloat16)

    def turn_own(i):
        if i == 0:
            load.wait()
        turn(xin[:, i * HALO:(i + 1) * HALO, :], HALO + i * HALO)

    def unit(rank, pair, first):
        p = places[Z][rank]
        lhs = xt[p, HALO - 1 - 2 * pair:HALO + window - 2 * pair].reshape((window + 1) * batch, width)
        part = jnp.dot(lhs, w[p, pair], preferred_element_type=jnp.float32)
        if first:
            acc[...] = part
        else:
            acc[...] += part

    work = [functools.partial(turn_own, i) for i in range(window // HALO)] + [functools.partial(turn_halo)]
    steps = []
    for rank in range(planes):
        for i in range(side_size):
            for j in range(side_size):
                for q in range(len(ORDERS)):
                    if (rank, i, j) != (0, 0, 0):
                        hops = (i > 0) + (j > 0)
                        steps.append((rank + HOP * hops, q, rank, i, j))
    steps.sort()
    of_plane = {rank: [step for step in steps if step[2] == rank] for rank in range(planes)}
    for _, q, rank, i, j in steps:
        process((rank, i, j), q)
        for _ in range(POPS if not (i and j) else LAST):
            if work:
                work.pop(0)()
        if (q, rank, i, j) == of_plane[rank][-1][1:]:
            for _, q, rank, i, j in of_plane[rank]:
                work.append(functools.partial(sibling_wait, (rank, i, j), q))
            work.extend(functools.partial(unit, rank, pair, rank == 0 and pair == 0) for pair in range(pairs))
    for item in work:
        item()

    total = (acc[batch:, :sensors] + acc[:window * batch, sensors:]).astype(jnp.bfloat16)
    for i in range(window // HALO):
        part = jnp.dot(to_batch, total[i * square:(i + 1) * square],
                       preferred_element_type=jnp.float32).astype(jnp.bfloat16)
        out_ref[:, i * HALO:(i + 1) * HALO, :] = part.reshape(batch, HALO, sensors)

    for cond, args in sends:
        if cond is None:
            copy(*args).wait_send()
        else:
            pl.when(cond)(lambda args=args: copy(*args).wait_send())
    pl.when(tm < n_tm - 1)(tail.wait_send)


def per_device(n_samp, n_tm, sources, operator, lag_order):
    batch, window, total_depth = sources.shape
    lags, depth, sensors = operator.shape
    side = math.isqrt(n_samp // 4)
    sizes = (n_samp // (side * side), side, side)
    width = side * side * depth
    return pl.pallas_call(
        functools.partial(fused, sizes, n_tm, lags),
        out_shape=jax.ShapeDtypeStruct((batch, window, sensors), jnp.bfloat16),
        in_specs=[
            pl.BlockSpec(memory_space=pl.ANY),
            pl.BlockSpec(memory_space=pltpu.VMEM),
            pl.BlockSpec(memory_space=pltpu.SMEM),
        ],
        out_specs=pl.BlockSpec(memory_space=pltpu.VMEM),
        scratch_shapes=[
            pltpu.VMEM((batch, window, total_depth), jnp.bfloat16),
            pltpu.VMEM((batch, HALO, total_depth), jnp.bfloat16),
            pltpu.VMEM((sizes[0], HALO + window, batch, width), jnp.bfloat16),
            pltpu.VMEM((sizes[0], lags // 2, width, 2 * sensors), jnp.bfloat16),
            pltpu.VMEM(((window + 1) * batch, 2 * sensors), jnp.float32),
            pltpu.SemaphoreType.DMA(()),
            pltpu.SemaphoreType.DMA(()),
            pltpu.SemaphoreType.DMA(()),
            pltpu.SemaphoreType.DMA((len(ORDERS), sum(sizes) - 2, n_samp)),
            pltpu.SemaphoreType.DMA((2, len(ORDERS), n_samp)),
        ],
        compiler_params=pltpu.CompilerParams(
            collective_id=0, has_side_effects=True, vmem_limit_bytes=48 << 20),
    )(sources, operator, lag_order)


def solution(mesh):
    placed = (P("samp", "tm", None), P(None, "samp", None), P())
    return jax.shard_map(
        functools.partial(per_device, mesh.shape["samp"], mesh.shape["tm"]),
        mesh=mesh, in_specs=placed, out_specs=P("samp", "tm", None), check_vma=False,
    )
```

time: 52.4 us -> 39.7 us (0.76)
  Pallas kernels: 47.8 us -> 35.6 us
    pallas_call x1, Pallas kernels: 47.8 us -> 35.6 us  [per_device(): pl.pallas_call(functools.partial(fused, sizes, n_tm, lags), out_shape=jax...]
where the time goes in v2:
time: 39.7 us; the launch traced here: 39.5 us
  Pallas kernels  35.6 us (90%)
  local copies, waits for them, and re-layouts  3.9 us (10%)
    pallas_call x1, Pallas kernels, per_device(): pl.pallas_call(functools.partial(fused, sizes, n_tm, lags), out_shape=jax...  35.6 us
    unnamed x7, local copies, waits for them, and re-layouts  3.9 us

profile of v2, /device:TPU:0, one launch (start us, length us, event | category | flops | bytes accessed | tf_op | source)
XLA Modules:
  0.0 39.5 jit_solution(15056693877785372590)
XLA Ops:
  0.0 0.0 copy-start
  0.0 1.6 %copy-done = bf16[16,64,1024]{2,1,0:T(8,128)(2,1)S(1)} copy-done((bf16[16,64,1024]{2,1,0:T(8,128)(2,1)S(1)}, bf16[16,64,1024]{2,1,0:T(8,128)(2,1)}, u32[]{:S(2)}) %copy-start) | copy-done | bytes 2097176
  1.6 0.0 copy-start.1
  1.6 0.9 %copy-done.1 = bf16[16,64,128]{2,1,0:T(8,128)(2,1)S(1)} copy-done((bf16[16,64,128]{2,1,0:T(8,128)(2,1)S(1)}, bf16[16,64,128]{2,1,0:T(8,128)(2,1)}, u32[]{:S(2)}) %copy-start.1) | copy-done | bytes 262168
  2.5 0.0 copy-start.2
  2.5 0.7 %copy-done.2 = s32[16]{0:T(128)S(1)} copy-done((s32[16]{0:T(128)S(1)}, s32[16]{0:T(128)}, u32[]{:S(2)}) %copy-start.2) | copy-done | bytes 88
  3.2 35.6 %shard_map.37 = bf16[16,64,128]{2,1,0:T(8,128)(2,1)S(1)} custom-call(bf16[16,64,1024]{2,1,0:T(8,128)(2,1)S(1)} %copy-done, bf16[16,64,128]{2,1,0:T(8,128)(2,1)S(1)} %copy-done.1, s32[16]{0:T(128)S(1)} %copy-done.2), custom_call_target="tpu_custom_call" | custom-call | tf_op jit(solution)/shard_map/pallas_call | solution.py:223
  38.8 0.7 %copy.5 = bf16[16,64,128]{2,1,0:T(8,128)(2,1)} copy(bf16[16,64,128]{2,1,0:T(8,128)(2,1)S(1)} %shard_map.37) | data formatting | bytes 524288
Async XLA Ops:
  0.0 1.6 %copy-start = (bf16[16,64,1024]{2,1,0:T(8,128)(2,1)S(1)}, bf16[16,64,1024]{2,1,0:T(8,128)(2,1)}, u32[]{:S(2)}) copy-start(bf16[16,64,1024]{2,1,0:T(8,128)(2,1)} %src_hbm.1) | copy-start | bytes 6291460
  1.6 0.9 %copy-start.1 = (bf16[16,64,128]{2,1,0:T(8,128)(2,1)S(1)}, bf16[16,64,128]{2,1,0:T(8,128)(2,1)}, u32[]{:S(2)}) copy-start(bf16[16,64,128]{2,1,0:T(8,128)(2,1)} %op_ref.1) | copy-start | bytes 786436
  2.5 0.7 %copy-start.2 = (s32[16]{0:T(128)S(1)}, s32[16]{0:T(128)}, u32[]{:S(2)}) copy-start(s32[16]{0:T(128)} %lag_ref.1) | copy-start | bytes 196

commit v3 on v2

--- a/solution.py
+++ b/solution.py
@@ -10,6 +10,7 @@
 
 MESH = pl.DeviceIdType.MESH
 HALO = 16
+GROUP = 4
 Z, A, B = 0, 1, 2
 ORDERS = ((Z, A, B),)
 SHARES = ((0, 4),)
@@ -170,8 +171,11 @@
 
     def unit(rank, pair, first):
         p = places[Z][rank]
-        lhs = xt[p, HALO - 1 - 2 * pair:HALO + window - 2 * pair].reshape((window + 1) * batch, width)
-        part = jnp.dot(lhs, w[p, pair], preferred_element_type=jnp.float32)
+        lhs = jnp.concatenate(
+            [xt[p, HALO - 1 - 2 * k:HALO + window - 2 * k].reshape((window + 1) * batch, width)
+             for k in range(pair, pair + GROUP)], axis=1)
+        rhs = w[p, pair:pair + GROUP].reshape(GROUP * width, 2 * sensors)
+        part = jnp.dot(lhs, rhs, preferred_element_type=jnp.float32)
         if first:
             acc[...] = part
         else:
@@ -196,7 +200,7 @@
         if (q, rank, i, j) == of_plane[rank][-1][1:]:
             for _, q, rank, i, j in of_plane[rank]:
                 work.append(functools.partial(sibling_wait, (rank, i, j), q))
-            work.extend(functools.partial(unit, rank, pair, rank == 0 and pair == 0) for pair in range(pairs))
+            work.extend(functools.partial(unit, rank, pair, rank == 0 and pair == 0) for pair in range(0, pairs, GROUP))
     for item in work:
         item()
 

time: 39.7 us -> 39.1 us (0.985)
  Pallas kernels: 35.6 us -> 35 us
    pallas_call x1, Pallas kernels: 35.6 us -> 35 us  [per_device(): pl.pallas_call(functools.partial(fused, sizes, n_tm, lags), out_shape=jax...]
where the time goes in v3:
time: 39.1 us; the launch traced here: 38.9 us
  Pallas kernels  35 us (90%)
  local copies, waits for them, and re-layouts  3.9 us (10%)
    pallas_call x1, Pallas kernels, per_device(): pl.pallas_call(functools.partial(fused, sizes, n_tm, lags), out_shape=jax...  35 us
    unnamed x7, local copies, waits for them, and re-layouts  3.9 us

profile of v3, /device:TPU:0, one launch (start us, length us, event | category | flops | bytes accessed | tf_op | source)
XLA Modules:
  0.0 38.9 jit_solution(11716384308603590475)
XLA Ops:
  0.0 0.0 copy-start
  0.0 1.6 %copy-done = bf16[16,64,1024]{2,1,0:T(8,128)(2,1)S(1)} copy-done((bf16[16,64,1024]{2,1,0:T(8,128)(2,1)S(1)}, bf16[16,64,1024]{2,1,0:T(8,128)(2,1)}, u32[]{:S(2)}) %copy-start) | copy-done | bytes 2097176
  1.6 0.0 copy-start.1
  1.6 0.9 %copy-done.1 = bf16[16,64,128]{2,1,0:T(8,128)(2,1)S(1)} copy-done((bf16[16,64,128]{2,1,0:T(8,128)(2,1)S(1)}, bf16[16,64,128]{2,1,0:T(8,128)(2,1)}, u32[]{:S(2)}) %copy-start.1) | copy-done | bytes 262168
  2.5 0.0 copy-start.2
  2.5 0.7 %copy-done.2 = s32[16]{0:T(128)S(1)} copy-done((s32[16]{0:T(128)S(1)}, s32[16]{0:T(128)}, u32[]{:S(2)}) %copy-start.2) | copy-done | bytes 88
  3.2 35.0 %shard_map.37 = bf16[16,64,128]{2,1,0:T(8,128)(2,1)S(1)} custom-call(bf16[16,64,1024]{2,1,0:T(8,128)(2,1)S(1)} %copy-done, bf16[16,64,128]{2,1,0:T(8,128)(2,1)S(1)} %copy-done.1, s32[16]{0:T(128)S(1)} %copy-done.2), custom_call_target="tpu_custom_call" | custom-call | tf_op jit(solution)/shard_map/pallas_call | solution.py:227
  38.2 0.7 %copy.5 = bf16[16,64,128]{2,1,0:T(8,128)(2,1)} copy(bf16[16,64,128]{2,1,0:T(8,128)(2,1)S(1)} %shard_map.37) | data formatting | bytes 524288
Async XLA Ops:
  0.0 1.6 %copy-start = (bf16[16,64,1024]{2,1,0:T(8,128)(2,1)S(1)}, bf16[16,64,1024]{2,1,0:T(8,128)(2,1)}, u32[]{:S(2)}) copy-start(bf16[16,64,1024]{2,1,0:T(8,128)(2,1)} %src_hbm.1) | copy-start | bytes 6291460
  1.6 0.9 %copy-start.1 = (bf16[16,64,128]{2,1,0:T(8,128)(2,1)S(1)}, bf16[16,64,128]{2,1,0:T(8,128)(2,1)}, u32[]{:S(2)}) copy-start(bf16[16,64,128]{2,1,0:T(8,128)(2,1)} %op_ref.1) | copy-start | bytes 786436
  2.5 0.7 %copy-start.2 = (s32[16]{0:T(128)S(1)}, s32[16]{0:T(128)}, u32[]{:S(2)}) copy-start(s32[16]{0:T(128)} %lag_ref.1) | copy-start | bytes 196
